TPU v7x, 32 devices: a whole 2x2x4 slice. The times are simulated.
32 devices in a mesh: grp: 2 (over x), res: 16 (over z, y, core).
Axes of the slice: x: 2, y: 2, z: 4, core: 2. Of those that a mesh axis runs over, the one named last changes fastest.
Arguments:
- alignment_activations: bfloat16 [128, 128, 256], P('grp', 'res'), parts along dimension 0, may hold values from -6 to 6
- projection_weight: bfloat16 [256, 64], replicated, may hold values from -0.375 to 0.375
- output_weight: bfloat16 [1024, 128], replicated, may hold values from -0.1875 to 0.1875
- output_bias: float32 [128], replicated, may hold values from -3 to 3
- pair_update_gradient: bfloat16 [256, 128, 128], P(('grp', 'res')), parts along dimension 0, may hold values from -6 to 6
- sequence_mask: int32 [128], P('grp'), parts along dimension 0, may hold values 0 or 1
- residue_mask: int32 [256], P('grp'), parts along dimension 0, may hold values 0 or 1
Outputs:
- pair_increment: bfloat16 [256, 128, 128], P(('grp', 'res')), parts along dimension 0
- alignment_gradient: bfloat16 [128, 128, 256], P('grp', 'res'), parts along dimension 0
There are 2 independent parts, one for each index of `grp`. A program takes and returns all parts, laid end to end along the dimension named above; an argument that names none is the same for every part. Nothing has to cross between parts.
All inputs are finite; a program needn't handle non-finite values.
Results may differ from a plain program's by a relative error of at most 0.007.
Values may be sent and summed in bfloat16 or wider, within the bound.
No kernel may reach another device: no remote copies, remote signals or barrier semaphores. Data moves between devices by JAX's collectives and lax.ppermute only.
A program may use at most 64 MiB of HBM per device.

v0:
```python
import jax
import jax.numpy as jnp
from jax import lax
from jax.sharding import PartitionSpec as P

eps_norm = 1e-05


def layer_norm_forward(values):
    mean_val = jnp.mean(values, axis=-1, keepdims=True)
    centered = values - mean_val
    inverse_deviation = lax.rsqrt(jnp.mean(centered * centered, axis=-1, keepdims=True) + eps_norm)
    return (centered * inverse_deviation, inverse_deviation)


def layer_norm_backward(grad_out, scaled_product, inverse_deviation):
    mean_grad = jnp.mean(grad_out, axis=-1, keepdims=True)
    mean_cross = jnp.mean(grad_out * scaled_product, axis=-1, keepdims=True)
    return inverse_deviation * (grad_out - mean_grad - scaled_product * mean_cross)


def body(
    alignment_activations,
    projection_weight,
    output_weight,
    output_bias,
    pair_update_gradient,
    sequence_mask,
    residue_mask,
):
    alignment_rows = alignment_activations.shape[0]
    local_rows = alignment_activations.shape[1]
    alignment_width = alignment_activations.shape[2]
    projected_width = projection_weight.shape[1] // 2
    pair_width = output_weight.shape[1]
    row_start = lax.axis_index("res") * local_rows
    residue_float_mask = residue_mask.astype(jnp.float32)
    local_residues = lax.dynamic_slice_in_dim(residue_float_mask, row_start, local_rows)
    alignment_mask = sequence_mask.astype(jnp.float32)[:, None] * local_residues[None, :]
    scaled_product, inverse_deviation = layer_norm_forward(
        alignment_activations.astype(jnp.float32)
    )
    normalized_input = scaled_product.astype(jnp.bfloat16)
    projected_rows = jnp.dot(
        normalized_input.reshape(-1, alignment_width),
        projection_weight,
        preferred_element_type=jnp.float32,
    )
    projected_rows = (
        projected_rows.reshape(alignment_rows, local_rows, 2 * projected_width)
        * alignment_mask[:, :, None]
    )
    projected_rows = projected_rows.astype(jnp.bfloat16)
    left_projected = projected_rows[:, :, :projected_width]
    right_proj = projected_rows[:, :, projected_width:]
    live_rows = jnp.sum(sequence_mask.astype(jnp.float32))
    right_all = lax.all_gather(right_proj, "res", axis=1, tiled=True)
    residue_count = right_all.shape[1]
    block_columns = 256 if residue_count % 256 == 0 else residue_count
    block_count = residue_count // block_columns
    count_rows = jnp.maximum(live_rows * local_residues[:, None] * residue_float_mask[None, :], 1.0)

    def pair_block(carry, block_id):
        pair_increment, left_gradient, gradient_pieces = carry
        column_offset = block_id * block_columns
        right_blk = lax.dynamic_slice_in_dim(right_all, column_offset, block_columns, 1)
        cot_blk = lax.dynamic_slice_in_dim(pair_update_gradient, column_offset, block_columns, 1)
        count_blk = lax.dynamic_slice_in_dim(count_rows, column_offset, block_columns, 1)
        outer = jnp.einsum(
            "sic,sjd->ijcd", left_projected, right_blk, preferred_element_type=jnp.float32
        )
        outer = outer.astype(jnp.bfloat16).reshape(-1, projected_width * projected_width)
        update = jnp.dot(outer, output_weight, preferred_element_type=jnp.float32)
        update = update.reshape(local_rows, block_columns, pair_width) + output_bias
        update = (update / count_blk[:, :, None]).astype(jnp.bfloat16)
        pair_increment = lax.dynamic_update_slice_in_dim(pair_increment, update, column_offset, 1)
        grad_outer = jnp.dot(
            cot_blk.reshape(-1, pair_width), output_weight.T, preferred_element_type=jnp.float32
        )
        grad_outer = (
            grad_outer.reshape(local_rows, block_columns, projected_width, projected_width)
            / count_blk[:, :, None, None]
        )
        grad_outer = grad_outer.astype(jnp.bfloat16)
        left_gradient = left_gradient + jnp.einsum(
            "ijcd,sjd->sic", grad_outer, right_blk, preferred_element_type=jnp.float32
        )
        gradient_piece = jnp.einsum(
            "ijcd,sic->jsd", grad_outer, left_projected, preferred_element_type=jnp.float32
        )
        gradient_pieces = lax.dynamic_update_slice_in_dim(
            gradient_pieces,
            gradient_piece.reshape(block_columns, alignment_rows * projected_width),
            column_offset,
            0,
        )
        return ((pair_increment, left_gradient, gradient_pieces), None)

    start_update = jnp.zeros((local_rows, residue_count, pair_width), jnp.bfloat16)
    initial_left = jnp.zeros((alignment_rows, local_rows, projected_width), jnp.float32)
    initial_pieces = jnp.zeros((residue_count, alignment_rows * projected_width), jnp.float32)
    (pair_increment, left_gradient, gradient_pieces), unused = lax.scan(
        pair_block, (start_update, initial_left, initial_pieces), jnp.arange(block_count)
    )
    gradient_total = lax.psum_scatter(gradient_pieces, "res", scatter_dimension=0, tiled=True)
    right_gradient = gradient_total.reshape(local_rows, alignment_rows, projected_width).transpose(
        1, 0, 2
    )
    projection_gradient = (
        jnp.concatenate([left_gradient, right_gradient], axis=-1) * alignment_mask[:, :, None]
    )
    projection_gradient = projection_gradient.astype(jnp.bfloat16)
    normalized_gradient = jnp.dot(
        projection_gradient.reshape(-1, 2 * projected_width),
        projection_weight.T,
        preferred_element_type=jnp.float32,
    )
    normalized_gradient = normalized_gradient.reshape(alignment_rows, local_rows, alignment_width)
    alignment_gradient = layer_norm_backward(
        normalized_gradient, scaled_product, inverse_deviation
    ).astype(jnp.bfloat16)
    return (pair_increment, alignment_gradient)


def solution(mesh):
    in_specs = (
        P("grp", "res", None),
        P(),
        P(),
        P(),
        P(("grp", "res"), None, None),
        P("grp"),
        P("grp"),
    )
    out_specs = (P(("grp", "res"), None, None), P("grp", "res", None))
    return jax.shard_map(body, mesh=mesh, in_specs=in_specs, out_specs=out_specs, check_vma=False)
```

profile of v0, /device:TPU:0, one launch (start us, length us, event | category | flops | bytes accessed | tf_op | source)
XLA Modules:
  0.0 89.6 jit_solution(17013610262894951195)
XLA Ops:
  7.2 1.3 %convert_reduce_fusion.1 = f32[]{:T(128)} fusion(s32[64]{0:T(128)} %param.12), kind=kLoop, calls=%fused_computation.46 | loop fusion | flops 127 | bytes 260 | tf_op jit(solution)/shard_map/reduce_sum | solution.py:56
  8.5 0.7 convert_element_type.41
  9.2 0.7 convert_element_type.42
  9.9 1.1 %convert_reduce_fusion = f32[64,8]{1,0:T(8,128)S(1)} fusion(bf16[64,8,256]{2,1,0:T(8,128)(2,1)} %param.7), kind=kLoop, calls=%fused_computation.15 | loop fusion | flops 261632 | bytes 264192 | tf_op jit(solution)/shard_map/reduce_sum | solution.py:10
  11.0 1.2 %fusion.23 = f32[64,8]{1,0:T(8,128)S(1)} fusion(bf16[64,8,256]{2,1,0:T(8,128)(2,1)} %param.7, f32[64,8]{1,0:T(8,128)S(1)} %broadcast_multiply_fusion.3), kind=kLoop, calls=%fused_computation.25 | loop fusion | flops 523776 | bytes 266240 | tf_op jit(solution)/shard_map/reduce_sum | solution.py:12
  12.2 0.7 broadcast_multiply_fusion.4
  13.0 0.6 copy-done.4
  13.6 1.3 %fusion.9 = bf16[64,8,64]{2,1,0:T(8,128)(2,1)S(1)} fusion(bf16[64,8,256]{2,1,0:T(8,128)(2,1)} %param.7, f32[64,8]{1,0:T(8,128)S(1)} %get-tuple-element.29, f32[64,8]{1,0:T(8,128)S(1)} %broadcast_multiply_fusion.3, f32[64,8]{1,0:T(8,128)S(1)} %get-tuple-element.40, bf16[256,64]{0,1:T(8,128)(2,1)} %param.8), kind=kOutput, calls=%fused_computation.11 | convolution fusion | flops 17367040 | bytes 366592 | tf_op jit(solution)/shard_map/dot_general | solution.py:44
  15.2 0.7 divide_convert_fusion
  15.9 0.8 fusion.4
  16.7 0.6 copy.30
  17.3 1.3 %copy.43 = f32[128,2048]{1,0:T(8,128)} copy(f32[128,2048]{0,1:T(8,128)S(1)} %bitcast.49) | data formatting | bytes 2097152
  18.7 32.3 %all_gather.3 = bf16[64,128,32]{2,1,0:T(8,128)(2,1)S(1)} all-gather(bf16[64,8,32]{2,1,0:T(8,128)(2,1)S(1)} %get-tuple-element.27), channel_id=1, replica_groups=mesh['grp'=2,'res'=16] {'res'}, dimensions={1}, use_global_device_ids=true | all-gather | bytes 557056 | tf_op jit(solution)/shard_map/all_gather | solution.py:57
  51.0 3.2 %copy.26 = bf16[64,128,32]{0,1,2:T(8,128)(2,1)S(1)} copy(bf16[64,128,32]{2,1,0:T(8,128)(2,1)S(1)} %all_gather.3) | data formatting | bytes 1048576 | tf_op jit(solution)/shard_map/all_gather | solution.py:57
  54.1 3.0 %fusion.10 = f32[64,8,32]{0,2,1:T(8,128)} fusion(bf16[8,128,32,32]{1,3,2,0:T(8,128)(2,1)} %copy-done.2, bf16[64,128,32]{0,1,2:T(8,128)(2,1)S(1)} %copy.26), kind=kOutput, calls=%fused_computation.12 | convolution fusion | flops 134217728 | bytes 2686976 | tf_op jit(solution)/shard_map/while/body/eval_jaxpr/ijcd,sjd->sic/dot_general | solution.py:85
  57.1 1.7 %copy.33 = f32[64,8,32]{2,1,0:T(8,128)} copy(f32[64,8,32]{0,2,1:T(8,128)} %fusion.10) | data formatting | bytes 131072 | tf_op jit(solution)/shard_map/while/body/eval_jaxpr/ijcd,sjd->sic/dot_general | solution.py:85
  58.9 3.2 %copy.34 = bf16[64,128,32,1]{0,1,3,2:T(8,128)(2,1)S(1)} copy(bf16[64,128,32,1]{2,1,0,3:T(8,128)(2,1)S(1)} %bitcast.47) | data formatting | bytes 1048576 | tf_op jit(solution)/shard_map/all_gather | solution.py:57
  62.1 0.7 convert_bitcast_fusion
  62.8 1.4 %copy.24 = bf16[8,128,32,32]{1,3,2,0:T(8,128)(2,1)S(1)} copy(bf16[8,128,32,32]{1,2,0,3:T(8,128)(2,1)S(1)} %convert_bitcast_fusion) | data formatting | bytes 4194304 | tf_op jit(solution)/shard_map/while/body/eval_jaxpr/convert_element_type | solution.py:72
  64.2 1.5 %fusion.8 = bf16[8,128,128]{2,1,0:T(8,128)(2,1)} fusion(bf16[8,128,1024]{1,2,0:T(8,128)(2,1)S(1)} %bitcast.50, bf16[1024,128]{1,0:T(8,128)(2,1)S(1)} %copy-done, f32[8,128]{1,0:T(8,128)S(1)} %multiply_maximum_fusion, f32[128]{0:T(128)S(1)} %copy-done.8), kind=kOutput, calls=%fused_computation.9 | convolution fusion | flops 268828672 | bytes 2626048 | tf_op jit(solution)/shard_map/while/body/eval_jaxpr/dot_general | solution.py:73
  65.7 14.0 %reduce-scatter.4.cloned.1.call-done = f32[8,2048]{1,0:T(8,128)} async-done(((f32[128,2048]{1,0:T(8,128)}), f32[8,2048]{1,0:T(8,128)}) %reduce-scatter.4.cloned.1.call-update) | async-done | bytes 65552
  79.7 1.2 %copy.44 = f32[8,2048]{0,1:T(8,128)S(1)} copy(f32[8,2048]{1,0:T(8,128)} %reduce-scatter.4.cloned.1.call-done) | data formatting | bytes 131072
  81.2 0.5 fusion.38
  81.8 1.0 %fusion.22 = bf16[64,8,256]{2,1,0:T(8,128)(2,1)} fusion(bf16[64,8,256]{2,1,0:T(8,128)(2,1)S(1)} %copy-done.1, f32[64,8,256]{2,1,0:T(8,128)S(1)} %get-tuple-element.28, f32[64,8]{1,0:T(8,128)S(1)} %broadcast_multiply_fusion.1, f32[64,8]{1,0:T(8,128)S(1)} %broadcast_multiply_fusion.2, f32[64,8]{1,0:T(8,128)S(1)} %get-tuple-element.29, ...), kind=kLoop, calls=%fused_computation.24 | loop fusion | flops 1048576 | bytes 1056768 | tf_op jit(solution)/shard_map/convert_element_type | solution.py:121
  (27 shorter events, 0.8 us)
Async XLA Ops:
  7.2 8.0 %copy-start = (bf16[1024,128]{1,0:T(8,128)(2,1)S(1)}, bf16[1024,128]{1,0:T(8,128)(2,1)}, u32[]{:S(2)}) copy-start(bf16[1024,128]{1,0:T(8,128)(2,1)} %param.9) | copy-start | bytes 786436
  7.2 8.0 %copy-start.7 = (bf16[8,128,128]{2,1,0:T(8,128)(2,1)S(1)}, bf16[8,128,128]{2,1,0:T(8,128)(2,1)}, u32[]{:S(2)}) copy-start(bf16[8,128,128]{2,1,0:T(8,128)(2,1)} %param.11) | copy-start | bytes 786436
  7.2 72.5 %reduce-scatter.4.cloned.1.call-start = ((), (), s32[]{:S(2)}) async-start(), calls=%async_computation.1 | async-start | bytes 1114112
  13.0 0.6 copy-start.4
  15.9 1.4 %copy-start.2 = (bf16[8,128,32,32]{1,3,2,0:T(8,128)(2,1)}, bf16[8,128,32,32]{1,3,2,0:T(8,128)(2,1)S(1)}, u32[]{:S(2)}) copy-start(bf16[8,128,32,32]{1,3,2,0:T(8,128)(2,1)S(1)} %divide_convert_fusion) | copy-start | bytes 6291460
  62.8 1.4 %copy-start.8 = (f32[128]{0:T(128)S(1)}, f32[128]{0:T(128)}, u32[]{:S(2)}) copy-start(f32[128]{0:T(128)} %param.10) | copy-start | bytes 1540
  65.6 15.5 %copy-start.1 = (bf16[64,8,256]{2,1,0:T(8,128)(2,1)S(1)}, bf16[64,8,256]{2,1,0:T(8,128)(2,1)}, u32[]{:S(2)}) copy-start(bf16[64,8,256]{2,1,0:T(8,128)(2,1)} %param.7) | copy-start | bytes 786436
  65.7 15.5 %copy-start.3 = (f32[64,8,32]{2,1,0:T(8,128)S(1)}, f32[64,8,32]{2,1,0:T(8,128)}, u32[]{:S(2)}) copy-start(f32[64,8,32]{2,1,0:T(8,128)} %copy.33) | copy-start | bytes 196612
  65.7 15.5 %copy-start.5 = (f32[64,8]{1,0:T(8,128)S(1)}, f32[64,8]{1,0:T(8,128)}, u32[]{:S(2)}) copy-start(f32[64,8]{1,0:T(8,128)} %copy-done.4) | copy-start | bytes 6148
  65.7 15.6 %copy-start.6 = (bf16[256,64]{0,1:T(8,128)(2,1)S(1)}, bf16[256,64]{0,1:T(8,128)(2,1)}, u32[]{:S(2)}) copy-start(bf16[256,64]{0,1:T(8,128)(2,1)} %param.8) | copy-start | bytes 98308
Sparse Core Ops, SparseCore 0:
  18.8 60.8 reduce-scatter.3
where the time goes:
time: 90 us; the launch traced here: 89.6 us
  blocking collectives  32.3 us (36%)
  between operations  14.2 us (16%)
  waiting for transfers between devices  14 us (16%)
  local copies, waits for them, and re-layouts  13.8 us (15%)
  matrix products  8.48 us (9%)
  other arithmetic  6.82 us (8%)
    all_gather x1, blocking collectives, body(): right_all = lax.all_gather(right_proj, 'res', axis=1, tiled=True)  32.3 us
    unnamed x2, waiting for transfers between devices  14 us
    all_gather x2, local copies, waits for them, and re-layouts, body(): right_all = lax.all_gather(right_proj, 'res', axis=1, tiled=True)  6.35 us
    unnamed x20, local copies, waits for them, and re-layouts  3.13 us
    dot_general x1, matrix products, pair_block(): jnp.einsum('ijcd,sjd->sic', grad_outer, right_blk, preferred_element_type...  2.99 us
  transfers between devices with their start and end apart: 1, of which 1 were waited for; matrix products, arithmetic and copies ran while one was open for 16% of the time, Pallas kernels for 0%

commit v1 on v0

--- a/solution.py
+++ b/solution.py
@@ -28,6 +28,21 @@
     sequence_mask,
     residue_mask,
 ):
+
+    def perform_groups(q_in):
+        now = lax.axis_size("res")
+        right_arr, part_now, found_now = (now, lax.axis_index("res"), q_in.shape[1])
+        inbox = [d * right_arr if it == 1 else d for it, d in enumerate(q_in.shape)]
+        clean = jnp.zeros(inbox, q_in.dtype)
+        w1 = lax.dynamic_update_slice_in_dim(clean, q_in, part_now * found_now, axis=1)
+        for dd in range(1, right_arr):
+            mat_out = list(map(lambda it: (it, (it + 1) % right_arr), range(right_arr)))
+            q_in = lax.ppermute(q_in, axis_name="res", perm=mat_out)
+            w1 = lax.dynamic_update_slice_in_dim(
+                w1, q_in, (part_now - dd) % right_arr * found_now, axis=1
+            )
+        return w1
+
     alignment_rows = alignment_activations.shape[0]
     local_rows = alignment_activations.shape[1]
     alignment_width = alignment_activations.shape[2]
@@ -54,7 +69,7 @@
     left_projected = projected_rows[:, :, :projected_width]
     right_proj = projected_rows[:, :, projected_width:]
     live_rows = jnp.sum(sequence_mask.astype(jnp.float32))
-    right_all = lax.all_gather(right_proj, "res", axis=1, tiled=True)
+    right_all = perform_groups(right_proj)
     residue_count = right_all.shape[1]
     block_columns = 256 if residue_count % 256 == 0 else residue_count
     block_count = residue_count // block_columns

time: 90 us -> 282 us (3.13)
  local copies, waits for them, and re-layouts: 13.8 us -> 151 us
  waiting for transfers between devices: 14 us -> 102 us
  blocking collectives: 32.3 us -> 0 us
    dynamic_update_slice x0 -> x16, local copies, waits for them, and re-layouts: none -> 115 us  [the longest x15 112 us: perform_groups(): lax.dynamic_update_slice_in_dim(w1, q_in, (part_now - dd) % right_arr * f...]
    ppermute x0 -> x15, waiting for transfers between devices: none -> 102 us  [perform_groups(): q_in = lax.ppermute(q_in, axis_name='res', perm=mat_out)]
    all_gather x1 -> x0, blocking collectives: 32.3 us -> none  [body(): right_all = lax.all_gather(right_proj, 'res', axis=1, tiled=True)]
    ppermute x0 -> x15, local copies, waits for them, and re-layouts: none -> 26.8 us  [perform_groups(): q_in = lax.ppermute(q_in, axis_name='res', perm=mat_out)]
    unnamed x2, waiting for transfers between devices: 14 us -> 0.02 us
    all_gather x2 -> x0, local copies, waits for them, and re-layouts: 6.35 us -> none  [body(): right_all = lax.all_gather(right_proj, 'res', axis=1, tiled=True)]
  transfers between devices with their start and end apart: 1 -> 16, of which waited for: 1 -> 14; matrix products, arithmetic and copies ran while one was open for 16% -> 53% of each run, Pallas kernels for 0% -> 0%
where the time goes in v1:
time: 282 us
  local copies, waits for them, and re-layouts  151 us (54%)
  waiting for transfers between devices  102 us (36%)
  between operations  14.9 us (5%)
  other arithmetic  6.82 us (2%)
  matrix products  6.16 us (2%)
    dynamic_update_slice x15, local copies, waits for them, and re-layouts, perform_groups(): lax.dynamic_update_slice_in_dim(w1, q_in, (part_now - dd) % right_arr * f...  112 us
    ppermute x15, waiting for transfers between devices, perform_groups(): q_in = lax.ppermute(q_in, axis_name='res', perm=mat_out)  102 us
    ppermute x15, local copies, waits for them, and re-layouts, perform_groups(): q_in = lax.ppermute(q_in, axis_name='res', perm=mat_out)  26.8 us
  transfers between devices with their start and end apart: 16, of which 14 were waited for; matrix products, arithmetic and copies ran while one was open for 53% of the time, Pallas kernels for 0%

profile of v1, /device:TPU:0, one launch (start us, length us, event | category | flops | bytes accessed | tf_op | source)
XLA Modules:
  0.0 281.6 jit_solution(12178421674492515662)
XLA Ops:
  19.9 8.0 %collective-permute-done = bf16[64,8,32]{2,1,0:T(8,128)(2,1)} collective-permute-done((bf16[64,8,32]{2,1,0:T(8,128)(2,1)}, bf16[64,8,32]{2,1,0:T(8,128)(2,1)}, u32[]{:S(2)}, u32[]{:S(2)}) %collective-permute-start) | collective-permute-done | bytes 32800 | tf_op jit(solution)/shard_map/ppermute | solution.py:40
  27.8 7.4 %collective-permute-done.1 = bf16[64,8,32]{2,1,0:T(8,128)(2,1)} collective-permute-done((bf16[64,8,32]{2,1,0:T(8,128)(2,1)}, bf16[64,8,32]{2,1,0:T(8,128)(2,1)}, u32[]{:S(2)}, u32[]{:S(2)}) %collective-permute-start.1) | collective-permute-done | bytes 32800 | tf_op jit(solution)/shard_map/ppermute | solution.py:40
  35.2 7.4 %collective-permute-done.2 = bf16[64,8,32]{2,1,0:T(8,128)(2,1)} collective-permute-done((bf16[64,8,32]{2,1,0:T(8,128)(2,1)}, bf16[64,8,32]{2,1,0:T(8,128)(2,1)}, u32[]{:S(2)}, u32[]{:S(2)}) %collective-permute-start.2) | collective-permute-done | bytes 32800 | tf_op jit(solution)/shard_map/ppermute | solution.py:40
  42.6 7.3 %collective-permute-done.3 = bf16[64,8,32]{2,1,0:T(8,128)(2,1)S(1)} collective-permute-done((bf16[64,8,32]{2,1,0:T(8,128)(2,1)}, bf16[64,8,32]{2,1,0:T(8,128)(2,1)S(1)}, u32[]{:S(2)}, u32[]{:S(2)}) %collective-permute-start.3) | collective-permute-done | bytes 32800 | tf_op jit(solution)/shard_map/ppermute | solution.py:40
  49.9 7.3 %collective-permute-done.4 = bf16[64,8,32]{2,1,0:T(8,128)(2,1)S(1)} collective-permute-done((bf16[64,8,32]{2,1,0:T(8,128)(2,1)S(1)}, bf16[64,8,32]{2,1,0:T(8,128)(2,1)S(1)}, u32[]{:S(2)}, u32[]{:S(2)}) %collective-permute-start.4) | collective-permute-done | bytes 32800 | tf_op jit(solution)/shard_map/ppermute | solution.py:40
  57.2 7.2 %collective-permute-done.5 = bf16[64,8,32]{2,1,0:T(8,128)(2,1)S(1)} collective-permute-done((bf16[64,8,32]{2,1,0:T(8,128)(2,1)S(1)}, bf16[64,8,32]{2,1,0:T(8,128)(2,1)S(1)}, u32[]{:S(2)}, u32[]{:S(2)}) %collective-permute-start.5) | collective-permute-done | bytes 32800 | tf_op jit(solution)/shard_map/ppermute | solution.py:40
  64.4 7.2 %collective-permute-done.6 = bf16[64,8,32]{2,1,0:T(8,128)(2,1)S(1)} collective-permute-done((bf16[64,8,32]{2,1,0:T(8,128)(2,1)S(1)}, bf16[64,8,32]{2,1,0:T(8,128)(2,1)S(1)}, u32[]{:S(2)}, u32[]{:S(2)}) %collective-permute-start.6) | collective-permute-done | bytes 32800 | tf_op jit(solution)/shard_map/ppermute | solution.py:40
  71.6 7.4 %collective-permute-done.7 = bf16[64,8,32]{2,1,0:T(8,128)(2,1)S(1)} collective-permute-done((bf16[64,8,32]{2,1,0:T(8,128)(2,1)S(1)}, bf16[64,8,32]{2,1,0:T(8,128)(2,1)S(1)}, u32[]{:S(2)}, u32[]{:S(2)}) %collective-permute-start.7) | collective-permute-done | bytes 32800 | tf_op jit(solution)/shard_map/ppermute | solution.py:40
  115.8 7.2 %collective-permute-done.13 = bf16[64,8,32]{2,1,0:T(8,128)(2,1)} collective-permute-done((bf16[64,8,32]{2,1,0:T(8,128)(2,1)S(1)}, bf16[64,8,32]{2,1,0:T(8,128)(2,1)}, u32[]{:S(2)}, u32[]{:S(2)}) %collective-permute-start.13) | collective-permute-done | bytes 32800 | tf_op jit(solution)/shard_map/ppermute | solution.py:40
  129.6 7.5 %dynamic_update_slice.53 = bf16[64,128,32]{1,0,2:T(8,128)(2,1)S(1)} dynamic-update-slice(bf16[64,128,32]{1,0,2:T(8,128)(2,1)S(1)} %dynamic_update_slice.52, bf16[64,8,32]{1,0,2:T(8,128)(2,1)S(1)} %copy.53, s32[]{:T(128)} %constant.128.clone.1, s32[]{:T(128)S(6)} %select_n.120, s32[]{:T(128)} %constant.128.clone.1) | dynamic-update-slice | bytes 65540 | tf_op jit(solution)/shard_map/dynamic_update_slice | solution.py:41
  138.9 7.5 %dynamic_update_slice.54 = bf16[64,128,32]{1,0,2:T(8,128)(2,1)S(1)} dynamic-update-slice(bf16[64,128,32]{1,0,2:T(8,128)(2,1)S(1)} %dynamic_update_slice.53, bf16[64,8,32]{1,0,2:T(8,128)(2,1)S(1)} %copy.54, s32[]{:T(128)} %constant.128.clone.1, s32[]{:T(128)S(6)} %select_n.122, s32[]{:T(128)} %constant.128.clone.1) | dynamic-update-slice | bytes 65540 | tf_op jit(solution)/shard_map/dynamic_update_slice | solution.py:41
  148.2 7.5 %dynamic_update_slice.55 = bf16[64,128,32]{1,0,2:T(8,128)(2,1)S(1)} dynamic-update-slice(bf16[64,128,32]{1,0,2:T(8,128)(2,1)S(1)} %dynamic_update_slice.54, bf16[64,8,32]{1,0,2:T(8,128)(2,1)S(1)} %copy.55, s32[]{:T(128)} %constant.128.clone.1, s32[]{:T(128)S(6)} %select_n.124, s32[]{:T(128)} %constant.128.clone.1) | dynamic-update-slice | bytes 65540 | tf_op jit(solution)/shard_map/dynamic_update_slice | solution.py:41
  157.4 7.5 %dynamic_update_slice.56 = bf16[64,128,32]{1,0,2:T(8,128)(2,1)S(1)} dynamic-update-slice(bf16[64,128,32]{1,0,2:T(8,128)(2,1)S(1)} %dynamic_update_slice.55, bf16[64,8,32]{1,0,2:T(8,128)(2,1)S(1)} %copy.56, s32[]{:T(128)} %constant.128.clone.1, s32[]{:T(128)S(6)} %select_n.126, s32[]{:T(128)} %constant.128.clone.1) | dynamic-update-slice | bytes 65540 | tf_op jit(solution)/shard_map/dynamic_update_slice | solution.py:41
  166.7 7.5 %dynamic_update_slice.57 = bf16[64,128,32]{1,0,2:T(8,128)(2,1)S(1)} dynamic-update-slice(bf16[64,128,32]{1,0,2:T(8,128)(2,1)S(1)} %dynamic_update_slice.56, bf16[64,8,32]{1,0,2:T(8,128)(2,1)S(1)} %copy.57, s32[]{:T(128)} %constant.128.clone.1, s32[]{:T(128)S(6)} %select_n.128, s32[]{:T(128)} %constant.128.clone.1) | dynamic-update-slice | bytes 65540 | tf_op jit(solution)/shard_map/dynamic_update_slice | solution.py:41
  175.9 7.5 %dynamic_update_slice.58 = bf16[64,128,32]{1,0,2:T(8,128)(2,1)S(1)} dynamic-update-slice(bf16[64,128,32]{1,0,2:T(8,128)(2,1)S(1)} %dynamic_update_slice.57, bf16[64,8,32]{1,0,2:T(8,128)(2,1)S(1)} %copy.58, s32[]{:T(128)} %constant.128.clone.1, s32[]{:T(128)S(6)} %select_n.130, s32[]{:T(128)} %constant.128.clone.1) | dynamic-update-slice | bytes 65540 | tf_op jit(solution)/shard_map/dynamic_update_slice | solution.py:41
  185.2 7.5 %dynamic_update_slice.59 = bf16[64,128,32]{1,0,2:T(8,128)(2,1)S(1)} dynamic-update-slice(bf16[64,128,32]{1,0,2:T(8,128)(2,1)S(1)} %dynamic_update_slice.58, bf16[64,8,32]{1,0,2:T(8,128)(2,1)S(1)} %copy.59, s32[]{:T(128)} %constant.128.clone.1, s32[]{:T(128)S(6)} %select_n.132, s32[]{:T(128)} %constant.128.clone.1) | dynamic-update-slice | bytes 65540 | tf_op jit(solution)/shard_map/dynamic_update_slice | solution.py:41
  194.4 7.7 %dynamic_update_slice.60 = bf16[64,128,32]{1,0,2:T(8,128)(2,1)S(1)} dynamic-update-slice(bf16[64,128,32]{1,0,2:T(8,128)(2,1)S(1)} %dynamic_update_slice.59, bf16[64,8,32]{1,0,2:T(8,128)(2,1)S(1)} %copy.60, s32[]{:T(128)} %constant.128.clone.1, s32[]{:T(128)S(6)} %select_n.134, s32[]{:T(128)} %constant.128.clone.1) | dynamic-update-slice | bytes 65540 | tf_op jit(solution)/shard_map/dynamic_update_slice | solution.py:41
  203.9 7.5 %dynamic_update_slice.61 = bf16[64,128,32]{1,0,2:T(8,128)(2,1)S(1)} dynamic-update-slice(bf16[64,128,32]{1,0,2:T(8,128)(2,1)S(1)} %dynamic_update_slice.60, bf16[64,8,32]{1,0,2:T(8,128)(2,1)S(1)} %copy.61, s32[]{:T(128)} %constant.128.clone.1, s32[]{:T(128)S(6)} %select_n.136, s32[]{:T(128)} %constant.128.clone.1) | dynamic-update-slice | bytes 65540 | tf_op jit(solution)/shard_map/dynamic_update_slice | solution.py:41
  213.2 7.5 %dynamic_update_slice.62 = bf16[64,128,32]{1,0,2:T(8,128)(2,1)S(1)} dynamic-update-slice(bf16[64,128,32]{1,0,2:T(8,128)(2,1)S(1)} %dynamic_update_slice.61, bf16[64,8,32]{1,0,2:T(8,128)(2,1)S(1)} %copy.62, s32[]{:T(128)} %constant.128.clone.1, s32[]{:T(128)S(6)} %select_n.138, s32[]{:T(128)} %constant.128.clone.1) | dynamic-update-slice | bytes 65540 | tf_op jit(solution)/shard_map/dynamic_update_slice | solution.py:41
  222.4 7.5 %dynamic_update_slice.63 = bf16[64,128,32]{1,0,2:T(8,128)(2,1)S(1)} dynamic-update-slice(bf16[64,128,32]{1,0,2:T(8,128)(2,1)S(1)} %dynamic_update_slice.62, bf16[64,8,32]{1,0,2:T(8,128)(2,1)S(1)} %copy.63, s32[]{:T(128)} %constant.128.clone.1, s32[]{:T(128)S(6)} %select_n.140, s32[]{:T(128)} %constant.128.clone.1) | dynamic-update-slice | bytes 65540 | tf_op jit(solution)/shard_map/dynamic_update_slice | solution.py:41
  231.7 7.5 %dynamic_update_slice.64 = bf16[64,128,32]{1,0,2:T(8,128)(2,1)S(1)} dynamic-update-slice(bf16[64,128,32]{1,0,2:T(8,128)(2,1)S(1)} %dynamic_update_slice.63, bf16[64,8,32]{1,0,2:T(8,128)(2,1)S(1)} %copy.64, s32[]{:T(128)} %constant.128.clone.1, s32[]{:T(128)S(6)} %select_n.142, s32[]{:T(128)} %constant.128.clone.1) | dynamic-update-slice | bytes 65540 | tf_op jit(solution)/shard_map/dynamic_update_slice | solution.py:41
  240.9 7.5 %dynamic_update_slice.65 = bf16[64,128,32]{1,0,2:T(8,128)(2,1)S(1)} dynamic-update-slice(bf16[64,128,32]{1,0,2:T(8,128)(2,1)S(1)} %dynamic_update_slice.64, bf16[64,8,32]{1,0,2:T(8,128)(2,1)S(1)} %copy.65, s32[]{:T(128)} %constant.128.clone.1, s32[]{:T(128)S(6)} %select_n.144, s32[]{:T(128)} %constant.128.clone.1) | dynamic-update-slice | bytes 65540 | tf_op jit(solution)/shard_map/dynamic_update_slice | solution.py:41
  250.2 7.5 %dynamic_update_slice.66 = bf16[64,128,32]{1,0,2:T(8,128)(2,1)S(1)} dynamic-update-slice(bf16[64,128,32]{1,0,2:T(8,128)(2,1)S(1)} %dynamic_update_slice.65, bf16[64,8,32]{1,0,2:T(8,128)(2,1)S(1)} %copy.66, s32[]{:T(128)} %constant.128.clone.1, s32[]{:T(128)S(6)} %select_n.146, s32[]{:T(128)} %constant.128.clone.1) | dynamic-update-slice | bytes 65540 | tf_op jit(solution)/shard_map/dynamic_update_slice | solution.py:41
  259.5 7.7 %dynamic_update_slice.67 = bf16[64,128,32]{1,0,2:T(8,128)(2,1)S(1)} dynamic-update-slice(bf16[64,128,32]{1,0,2:T(8,128)(2,1)S(1)} %dynamic_update_slice.66, bf16[64,8,32]{1,0,2:T(8,128)(2,1)S(1)} %copy.67, s32[]{:T(128)} %constant.128.clone.1, s32[]{:T(128)S(6)} %select_n.148, s32[]{:T(128)} %constant.128.clone.1) | dynamic-update-slice | bytes 65540 | tf_op jit(solution)/shard_map/dynamic_update_slice | solution.py:41
  (103 shorter events, 88.0 us)
Async XLA Ops:
  7.2 264.5 %reduce-scatter.4.cloned.1.call-start = ((), (), s32[]{:S(2)}) async-start(), calls=%async_computation.1 | async-start | bytes 1114112
  19.3 8.5 %collective-permute-start = (bf16[64,8,32]{2,1,0:T(8,128)(2,1)}, bf16[64,8,32]{2,1,0:T(8,128)(2,1)}, u32[]{:S(2)}, u32[]{:S(2)}) collective-permute-start(bf16[64,8,32]{2,1,0:T(8,128)(2,1)} %get-tuple-element.27), channel_id=1, source_target_pairs={{0,1},{1,2},{2,3},{3,4},{4,5},{5,6},{6,7},{7,8},{8,9},{9,10},{10,1... | collective-permute-start | bytes 98312 | tf_op jit(solution)/shard_map/ppermute | solution.py:40
  27.8 7.4 %collective-permute-start.1 = (bf16[64,8,32]{2,1,0:T(8,128)(2,1)}, bf16[64,8,32]{2,1,0:T(8,128)(2,1)}, u32[]{:S(2)}, u32[]{:S(2)}) collective-permute-start(bf16[64,8,32]{2,1,0:T(8,128)(2,1)} %collective-permute-done), channel_id=1, source_target_pairs={{0,1},{1,2},{2,3},{3,4},{4,5},{5,6},{6,7},{7,8},{8,9},{9,10},{10,1... | collective-permute-start | bytes 98312 | tf_op jit(solution)/shard_map/ppermute | solution.py:40
  35.2 7.4 %collective-permute-start.2 = (bf16[64,8,32]{2,1,0:T(8,128)(2,1)}, bf16[64,8,32]{2,1,0:T(8,128)(2,1)}, u32[]{:S(2)}, u32[]{:S(2)}) collective-permute-start(bf16[64,8,32]{2,1,0:T(8,128)(2,1)} %collective-permute-done.1), channel_id=1, source_target_pairs={{0,1},{1,2},{2,3},{3,4},{4,5},{5,6},{6,7},{7,8},{8,9},{9,10},{10,1... | collective-permute-start | bytes 98312 | tf_op jit(solution)/shard_map/ppermute | solution.py:40
  42.6 7.3 %collective-permute-start.3 = (bf16[64,8,32]{2,1,0:T(8,128)(2,1)}, bf16[64,8,32]{2,1,0:T(8,128)(2,1)S(1)}, u32[]{:S(2)}, u32[]{:S(2)}) collective-permute-start(bf16[64,8,32]{2,1,0:T(8,128)(2,1)} %collective-permute-done.2), channel_id=1, source_target_pairs={{0,1},{1,2},{2,3},{3,4},{4,5},{5,6},{6,7},{7,8},{8,9},{9,10},{10,1... | collective-permute-start | bytes 98312 | tf_op jit(solution)/shard_map/ppermute | solution.py:40
  49.9 73.1 %copy-start.2 = (bf16[64,8,32]{2,1,0:T(8,128)(2,1)}, bf16[64,8,32]{2,1,0:T(8,128)(2,1)S(1)}, u32[]{:S(2)}) copy-start(bf16[64,8,32]{2,1,0:T(8,128)(2,1)S(1)} %collective-permute-done.3) | copy-start | bytes 98308
  49.9 7.3 %collective-permute-start.4 = (bf16[64,8,32]{2,1,0:T(8,128)(2,1)S(1)}, bf16[64,8,32]{2,1,0:T(8,128)(2,1)S(1)}, u32[]{:S(2)}, u32[]{:S(2)}) collective-permute-start(bf16[64,8,32]{2,1,0:T(8,128)(2,1)S(1)} %collective-permute-done.3), channel_id=1, source_target_pairs={{0,1},{1,2},{2,3},{3,4},{4,5},{5,6},{6,7},{7,8},{8,9},{9,10},{10,1... | collective-permute-start | bytes 98312 | tf_op jit(solution)/shard_map/ppermute | solution.py:40
  57.2 65.8 %copy-start.3 = (bf16[64,8,32]{2,1,0:T(8,128)(2,1)}, bf16[64,8,32]{2,1,0:T(8,128)(2,1)S(1)}, u32[]{:S(2)}) copy-start(bf16[64,8,32]{2,1,0:T(8,128)(2,1)S(1)} %collective-permute-done.4) | copy-start | bytes 98308
  57.2 7.2 %collective-permute-start.5 = (bf16[64,8,32]{2,1,0:T(8,128)(2,1)S(1)}, bf16[64,8,32]{2,1,0:T(8,128)(2,1)S(1)}, u32[]{:S(2)}, u32[]{:S(2)}) collective-permute-start(bf16[64,8,32]{2,1,0:T(8,128)(2,1)S(1)} %collective-permute-done.4), channel_id=1, source_target_pairs={{0,1},{1,2},{2,3},{3,4},{4,5},{5,6},{6,7},{7,8},{8,9},{9,10},{10,1... | collective-permute-start | bytes 98312 | tf_op jit(solution)/shard_map/ppermute | solution.py:40
  64.4 58.6 %copy-start.4 = (bf16[64,8,32]{2,1,0:T(8,128)(2,1)}, bf16[64,8,32]{2,1,0:T(8,128)(2,1)S(1)}, u32[]{:S(2)}) copy-start(bf16[64,8,32]{2,1,0:T(8,128)(2,1)S(1)} %collective-permute-done.5) | copy-start | bytes 98308
  64.4 7.2 %collective-permute-start.6 = (bf16[64,8,32]{2,1,0:T(8,128)(2,1)S(1)}, bf16[64,8,32]{2,1,0:T(8,128)(2,1)S(1)}, u32[]{:S(2)}, u32[]{:S(2)}) collective-permute-start(bf16[64,8,32]{2,1,0:T(8,128)(2,1)S(1)} %collective-permute-done.5), channel_id=1, source_target_pairs={{0,1},{1,2},{2,3},{3,4},{4,5},{5,6},{6,7},{7,8},{8,9},{9,10},{10,1... | collective-permute-start | bytes 98312 | tf_op jit(solution)/shard_map/ppermute | solution.py:40
  71.6 51.4 %copy-start.5 = (bf16[64,8,32]{2,1,0:T(8,128)(2,1)}, bf16[64,8,32]{2,1,0:T(8,128)(2,1)S(1)}, u32[]{:S(2)}) copy-start(bf16[64,8,32]{2,1,0:T(8,128)(2,1)S(1)} %collective-permute-done.6) | copy-start | bytes 98308
  71.6 7.4 %collective-permute-start.7 = (bf16[64,8,32]{2,1,0:T(8,128)(2,1)S(1)}, bf16[64,8,32]{2,1,0:T(8,128)(2,1)S(1)}, u32[]{:S(2)}, u32[]{:S(2)}) collective-permute-start(bf16[64,8,32]{2,1,0:T(8,128)(2,1)S(1)} %collective-permute-done.6), channel_id=1, source_target_pairs={{0,1},{1,2},{2,3},{3,4},{4,5},{5,6},{6,7},{7,8},{8,9},{9,10},{10,1... | collective-permute-start | bytes 98312 | tf_op jit(solution)/shard_map/ppermute | solution.py:40
  79.0 46.1 %copy-start.6 = (bf16[64,8,32]{2,1,0:T(8,128)(2,1)}, bf16[64,8,32]{2,1,0:T(8,128)(2,1)S(1)}, u32[]{:S(2)}) copy-start(bf16[64,8,32]{2,1,0:T(8,128)(2,1)S(1)} %collective-permute-done.7) | copy-start | bytes 98308
  79.0 7.1 %collective-permute-start.8 = (bf16[64,8,32]{2,1,0:T(8,128)(2,1)S(1)}, bf16[64,8,32]{2,1,0:T(8,128)(2,1)S(1)}, u32[]{:S(2)}, u32[]{:S(2)}) collective-permute-start(bf16[64,8,32]{2,1,0:T(8,128)(2,1)S(1)} %collective-permute-done.7), channel_id=1, source_target_pairs={{0,1},{1,2},{2,3},{3,4},{4,5},{5,6},{6,7},{7,8},{8,9},{9,10},{10,1... | collective-permute-start | bytes 98312 | tf_op jit(solution)/shard_map/ppermute | solution.py:40
  86.1 39.0 %copy-start.7 = (bf16[64,8,32]{2,1,0:T(8,128)(2,1)}, bf16[64,8,32]{2,1,0:T(8,128)(2,1)S(1)}, u32[]{:S(2)}) copy-start(bf16[64,8,32]{2,1,0:T(8,128)(2,1)S(1)} %collective-permute-done.8) | copy-start | bytes 98308
  86.1 7.1 %collective-permute-start.9 = (bf16[64,8,32]{2,1,0:T(8,128)(2,1)S(1)}, bf16[64,8,32]{2,1,0:T(8,128)(2,1)S(1)}, u32[]{:S(2)}, u32[]{:S(2)}) collective-permute-start(bf16[64,8,32]{2,1,0:T(8,128)(2,1)S(1)} %collective-permute-done.8), channel_id=1, source_target_pairs={{0,1},{1,2},{2,3},{3,4},{4,5},{5,6},{6,7},{7,8},{8,9},{9,10},{10,1... | collective-permute-start | bytes 98312 | tf_op jit(solution)/shard_map/ppermute | solution.py:40
  93.2 31.9 %copy-start.8 = (bf16[64,8,32]{2,1,0:T(8,128)(2,1)}, bf16[64,8,32]{2,1,0:T(8,128)(2,1)S(1)}, u32[]{:S(2)}) copy-start(bf16[64,8,32]{2,1,0:T(8,128)(2,1)S(1)} %collective-permute-done.9) | copy-start | bytes 98308
  93.2 7.1 %collective-permute-start.10 = (bf16[64,8,32]{2,1,0:T(8,128)(2,1)S(1)}, bf16[64,8,32]{2,1,0:T(8,128)(2,1)S(1)}, u32[]{:S(2)}, u32[]{:S(2)}) collective-permute-start(bf16[64,8,32]{2,1,0:T(8,128)(2,1)S(1)} %collective-permute-done.9), channel_id=1, source_target_pairs={{0,1},{1,2},{2,3},{3,4},{4,5},{5,6},{6,7},{7,8},{8,9},{9,10},{10,1... | collective-permute-start | bytes 98312 | tf_op jit(solution)/shard_map/ppermute | solution.py:40
  100.3 24.8 %copy-start.9 = (bf16[64,8,32]{2,1,0:T(8,128)(2,1)}, bf16[64,8,32]{2,1,0:T(8,128)(2,1)S(1)}, u32[]{:S(2)}) copy-start(bf16[64,8,32]{2,1,0:T(8,128)(2,1)S(1)} %collective-permute-done.10) | copy-start | bytes 98308
  100.3 7.1 %collective-permute-start.11 = (bf16[64,8,32]{2,1,0:T(8,128)(2,1)S(1)}, bf16[64,8,32]{2,1,0:T(8,128)(2,1)S(1)}, u32[]{:S(2)}, u32[]{:S(2)}) collective-permute-start(bf16[64,8,32]{2,1,0:T(8,128)(2,1)S(1)} %collective-permute-done.10), channel_id=1, source_target_pairs={{0,1},{1,2},{2,3},{3,4},{4,5},{5,6},{6,7},{7,8},{8,9},{9,10},{10,1... | collective-permute-start | bytes 98312 | tf_op jit(solution)/shard_map/ppermute | solution.py:40
  108.1 7.1 %collective-permute-start.12 = (bf16[64,8,32]{2,1,0:T(8,128)(2,1)S(1)}, bf16[64,8,32]{2,1,0:T(8,128)(2,1)S(1)}, u32[]{:S(2)}, u32[]{:S(2)}) collective-permute-start(bf16[64,8,32]{2,1,0:T(8,128)(2,1)S(1)} %collective-permute-done.11), channel_id=1, source_target_pairs={{0,1},{1,2},{2,3},{3,4},{4,5},{5,6},{6,7},{7,8},{8,9},{9,10},{10,1... | collective-permute-start | bytes 98312 | tf_op jit(solution)/shard_map/ppermute | solution.py:40
  115.8 7.2 %collective-permute-start.13 = (bf16[64,8,32]{2,1,0:T(8,128)(2,1)S(1)}, bf16[64,8,32]{2,1,0:T(8,128)(2,1)}, u32[]{:S(2)}, u32[]{:S(2)}) collective-permute-start(bf16[64,8,32]{2,1,0:T(8,128)(2,1)S(1)} %collective-permute-done.12), channel_id=1, source_target_pairs={{0,1},{1,2},{2,3},{3,4},{4,5},{5,6},{6,7},{7,8},{8,9},{9,10},{10,1... | collective-permute-start | bytes 98312 | tf_op jit(solution)/shard_map/ppermute | solution.py:40
  123.0 134.7 %collective-permute-start.14 = (bf16[64,8,32]{2,1,0:T(8,128)(2,1)}, bf16[64,8,32]{2,1,0:T(8,128)(2,1)}, u32[]{:S(2)}, u32[]{:S(2)}) collective-permute-start(bf16[64,8,32]{2,1,0:T(8,128)(2,1)} %collective-permute-done.13), channel_id=1, source_target_pairs={{0,1},{1,2},{2,3},{3,4},{4,5},{5,6},{6,7},{7,8},{8,9},{9,10},{10,1... | collective-permute-start | bytes 98312 | tf_op jit(solution)/shard_map/ppermute | solution.py:40
  (9 other events, 25.2 us)
Sparse Core Ops, SparseCore 0:
  19.4 61.7 reduce-scatter.3
